TPU v7x, 32 devices: a whole 2x2x4 slice. The times are simulated.
32 devices in a mesh: row: 2 (over y), col: 16 (over z, x, core).
Axes of the slice: x: 2, y: 2, z: 4, core: 2. Of those that a mesh axis runs over, the one named last changes fastest.
Arguments:
- blocks: bfloat16 [128, 2048, 128], P('row', 'col'), may hold values from -0.1875 to 0.1875
- block_rows: int32 [2, 1024], P('row', 'col'), may hold values from 0 to 2047, as said below
- block_cols: int32 [2, 1024], P('row', 'col'), may hold values from 0 to 255
- counts: int32 [2, 16], P('row', 'col'), may hold values from 1 to 64, as said below
- start_vectors: float32 [32, 524288], P(None, ('row', 'col')), may hold values from -6 to 6
Outputs:
- vectors: float32 [32, 524288], P(None, ('row', 'col'))
Inputs may be any that keep to these rules, and one draw needn't show every extreme that they name: counts[r, c] is the number of live slots of grid position (r, c); in every draw some position has all 64 slots live. For every grid position (r, c) and every o < 16, exactly 4 of its 64 slots have block_rows[r, c * 64 + s] // 128 == o.
All inputs are finite; a program needn't handle non-finite values.
Results may differ from a plain program's by a relative error of at most 0.0036.
Values may be sent and summed in bfloat16 or wider, within the bound.
A program may use at most 256 MiB of HBM per device.

v0:
```python
import math
import jax
import jax.numpy as jnp
from jax import lax
from jax.sharding import PartitionSpec as P

N = 524288
ITERS = 2


def cholesky_lower(gram_matrix):
    matrix_order = gram_matrix.shape[0]
    positions = jnp.arange(matrix_order)

    def column_step(position, factor):
        before = (positions < position).astype(gram_matrix.dtype)
        target_row = lax.dynamic_index_in_dim(factor, position, 0, keepdims=False) * before
        column = lax.dynamic_index_in_dim(gram_matrix, position, 1, keepdims=False)
        residue = column - jnp.sum(factor * target_row[None, :], axis=1)
        on_diagonal = positions == position
        pivot_value = jnp.sqrt(jnp.sum(jnp.where(on_diagonal, residue, 0.0)))
        values = jnp.where(on_diagonal, pivot_value, residue / pivot_value)
        values = jnp.where(positions >= position, values, 0.0)
        return lax.dynamic_update_index_in_dim(factor, values, position, 1)

    return lax.fori_loop(0, matrix_order, column_step, jnp.zeros_like(gram_matrix))


def lower_inverse(lower_factor):
    matrix_order = lower_factor.shape[0]
    positions = jnp.arange(matrix_order)

    def row_step(position, inverse):
        lower_row = lax.dynamic_index_in_dim(lower_factor, position, 0, keepdims=False)
        before = (positions < position).astype(lower_factor.dtype)
        inner_sum = jnp.sum((lower_row * before)[:, None] * inverse, axis=0)
        unit_row = (positions == position).astype(lower_factor.dtype)
        pivot_value = jnp.sum(lower_row * unit_row)
        return lax.dynamic_update_index_in_dim(
            inverse, (unit_row - inner_sum) / pivot_value, position, 0
        )

    return lax.fori_loop(0, matrix_order, row_step, jnp.zeros_like(lower_factor))


def accumulate(blocks, rows_index, cols_index, live_count, row_panel, col_panel):
    slot_count, block_size = (blocks.shape[0], blocks.shape[1])
    vector_count = row_panel.shape[0]
    row_blocks = row_panel.reshape(vector_count, -1, block_size)
    col_blocks = col_panel.reshape(vector_count, -1, block_size)
    group_size = math.gcd(slot_count, 64)
    turn_count = (live_count + group_size - 1) // group_size
    slot_offsets = jnp.arange(group_size, dtype=jnp.int32)

    def one_group(turn_index, partial_sums):
        row_sums, col_sums = partial_sums
        first_slot = turn_index * group_size
        live_mask = (first_slot + slot_offsets < live_count).astype(jnp.float32)
        from_cols = jnp.take(col_blocks, cols_index, axis=1)
        from_rows = jnp.take(row_blocks, rows_index, axis=1)
        to_cols = jnp.einsum("kgi,gij->kgj", from_rows, blocks, preferred_element_type=jnp.float32)
        col_sums = col_sums.at[:, cols_index].add(to_cols * live_mask[None, :, None])
        to_rows = jnp.einsum("kgj,gij->kgi", from_cols, blocks, preferred_element_type=jnp.float32)
        row_sums = row_sums.at[:, rows_index].add(to_rows * live_mask[None, :, None])
        return (row_sums, col_sums)

    row_start = jnp.zeros(row_blocks.shape, jnp.float32)
    initial = (row_start, jnp.zeros(col_blocks.shape, jnp.float32))
    return lax.fori_loop(0, turn_count, one_group, initial)


def per_device(blocks, block_rows, block_cols, counts, start_vectors):
    live_count = counts[0, 0]
    rows_index = block_rows[0]
    cols_index = block_cols[0]
    vectors = start_vectors
    for iteration in range(ITERS):
        rounded = vectors.astype(jnp.bfloat16)
        vector_count = rounded.shape[0]
        col_panel = lax.all_gather(rounded, "row", axis=1, tiled=True)
        row_panel = lax.all_gather(rounded, "col", axis=1, tiled=True)
        row_sums, col_sums = accumulate(
            blocks, rows_index, cols_index, live_count, row_panel, col_panel
        )
        from_row_group = lax.psum_scatter(
            row_sums.reshape(vector_count, -1), "col", scatter_dimension=1, tiled=True
        )
        from_col_group = lax.psum_scatter(
            col_sums.reshape(vector_count, -1), "row", scatter_dimension=1, tiled=True
        )
        product = from_row_group + from_col_group
        local_gram = jnp.dot(
            product, product.T, precision=lax.Precision.HIGHEST, preferred_element_type=jnp.float32
        )
        gram_matrix = lax.psum(local_gram, ("row", "col")) / N
        inverse = lower_inverse(cholesky_lower(gram_matrix))
        vectors = jnp.dot(
            inverse, product, precision=lax.Precision.HIGHEST, preferred_element_type=jnp.float32
        )
    return vectors


def solution(mesh):
    placed = (
        P("row", "col", None),
        P("row", "col"),
        P("row", "col"),
        P("row", "col"),
        P(None, ("row", "col")),
    )
    return jax.shard_map(
        per_device, mesh=mesh, in_specs=placed, out_specs=P(None, ("row", "col")), check_vma=False
    )
```

profile of v0, /device:TPU:0, one launch (start us, length us, event | category | flops | bytes accessed | tf_op | source)
XLA Modules:
  0.0 1549.7 jit_solution(5209276909103308987)
XLA Ops:
  6.5 2.8 convert_element_type.66
  9.4 0.7 all-gather.7.cloned.1.call-update
  11.0 34.4 %all-gather.5.cloned.1.call-done = bf16[32,32768]{1,0:T(8,128)(2,1)} async-done(((bf16[32,16384]{1,0:T(8,128)(2,1)}), bf16[32,32768]{1,0:T(8,128)(2,1)}) %all-gather.5.cloned.1.call-update) | async-done | bytes 2097168 | tf_op jit(solution)/shard_map/all_gather | solution.py:80
  45.4 3.3 copy_bitcast_fusion.7
  48.6 2.2 gather_fusion
  50.9 2.2 fusion.34
  53.1 121.4 %all-gather.7.cloned.1.call-done = bf16[32,262144]{1,0:T(8,128)(2,1)} async-done(((bf16[32,16384]{1,0:T(8,128)(2,1)}), bf16[32,262144]{1,0:T(8,128)(2,1)}) %all-gather.7.cloned.1.call-update) | async-done | bytes 16777232 | tf_op jit(solution)/shard_map/all_gather | solution.py:81
  174.5 14.5 copy_bitcast_fusion.3
  189.0 6.4 gather_fusion.1
  195.4 1.7 fusion.32
  197.1 11.3 broadcast.314.clone
  208.4 2.6 broadcast.315.clone
  210.9 20.4 %while.90 = (s32[]{:T(128)}, f32[32,2048,128]{2,0,1:T(8,128)}, f32[32,256,128]{2,0,1:T(8,128)}, s32[]{:T(128)}, s32[64]{0:T(128)S(1)}, /*index=5*/s32[]{:T(128)}...) while((s32[]{:T(128)}, f32[32,2048,128]{2,0,1:T(8,128)}, ...), condition=%wide.region_3.6_spmd.clone, body=%wide.region_0.5_spmd.clone.sunk | while | flops 1049155 | bytes 10487937 | solution.py:69
  211.6 2.7 broadcast_multiply_fusion.8
  214.3 9.0 scatter_fusion
  223.3 8.0 scatter_fusion.1
  231.3 4.4 copy_bitcast_fusion.5
  235.8 22.6 %copy_bitcast_fusion.1 = f32[32,262144]{1,0:T(8,128)} fusion(f32[32,2048,128]{2,0,1:T(8,128)} %get-tuple-element.609), kind=kLoop, calls=%fused_computation.69 | loop fusion | bytes 67108864 | tf_op jit(solution)/shard_map/reshape | solution.py:86
  258.5 30.0 %reduce-scatter.7.cloned.1.call-done = f32[32,16384]{1,0:T(8,128)} async-done(((f32[32,32768]{1,0:T(8,128)}), f32[32,16384]{1,0:T(8,128)}) %reduce-scatter.7.cloned.1.call-update) | async-done | bytes 2097168 | tf_op jit(solution)/shard_map/reduce_scatter | solution.py:88
  288.4 337.4 %reduce-scatter.5.cloned.1.call-done = f32[32,16384]{1,0:T(8,128)} async-done(((f32[32,262144]{1,0:T(8,128)}), f32[32,16384]{1,0:T(8,128)}) %reduce-scatter.5.cloned.1.call-update) | async-done | bytes 2097168 | tf_op jit(solution)/shard_map/reduce_scatter | solution.py:85
  625.8 2.4 add.220
  628.2 1.3 copy-done.2
  629.5 1.8 fusion.52
  631.3 39.1 %psum.14 = f32[32,32]{1,0:T(8,128)S(1)} all-reduce(f32[32,32]{1,0:T(8,128)S(1)} %fusion.52), channel_id=1, replica_groups=mesh['row'=2,'col'=16] {'row','col'}, use_global_device_ids=true, to_apply=%region_6.9 | all-reduce | flops 1024 | bytes 8192 | tf_op jit(solution)/shard_map/psum | solution.py:95
  670.4 58.1 %while.92 = (s32[]{:T(128)}, f32[32,32]{1,0:T(8,128)S(1)}, f32[32,32]{0,1:T(8,128)S(1)}, s32[]{:T(128)}, s32[]{:T(128)}) while((s32[]{:T(128)}, f32[32,32]{1,0:T(8,128)S(1)}, f32[32,32]{0,1:T(8,128)S(1)}, s32[]{:T(128)}, s32[]{:T(128)}) %tuple.192), condition=%wide.region_10.13_spmd.clone.clone, body=%wide.region_7.12_spmd.clone.clone.sunk | while | flops 2401 | bytes 8913 | solution.py:26
  670.6 0.7 fusion.88
  672.3 0.7 fusion.88
  674.1 0.7 fusion.88
  676.0 0.7 fusion.88
  677.8 0.7 fusion.88
  679.6 0.7 fusion.88
  685.1 0.7 fusion.88
  690.5 0.7 fusion.88
  708.7 0.7 fusion.88
  714.2 0.7 fusion.88
  719.6 0.7 fusion.88
  725.1 0.7 fusion.88
  728.6 49.0 %while.93 = (s32[]{:T(128)}, f32[32,32]{1,0:T(8,128)S(1)}, f32[32,32]{1,0:T(8,128)S(1)}, s32[]{:T(128)}, s32[]{:T(128)}) while((s32[]{:T(128)}, f32[32,32]{1,0:T(8,128)S(1)}, f32[32,32]{1,0:T(8,128)S(1)}, s32[]{:T(128)}, s32[]{:T(128)}) %tuple.195), condition=%wide.region_14.17_spmd.clone.clone, body=%wide.region_11.16_spmd.clone.clone.sunk | while | flops 2305 | bytes 6221 | solution.py:43
  777.6 4.4 convolution_convert_fusion
  782.8 32.2 %all-gather.9.cloned.1.call-done = bf16[32,32768]{1,0:T(8,128)(2,1)} async-done(((bf16[32,16384]{1,0:T(8,128)(2,1)}), bf16[32,32768]{1,0:T(8,128)(2,1)}) %all-gather.9.cloned.1.call-update) | async-done | bytes 2097168 | tf_op jit(solution)/shard_map/all_gather | solution.py:80
  815.1 3.3 copy_bitcast_fusion.6
  818.3 2.2 gather_fusion.2
  820.6 2.2 fusion.30
  822.8 121.5 %all-gather.11.cloned.1.call-done = bf16[32,262144]{1,0:T(8,128)(2,1)} async-done(((bf16[32,16384]{1,0:T(8,128)(2,1)}), bf16[32,262144]{1,0:T(8,128)(2,1)}) %all-gather.11.cloned.1.call-update) | async-done | bytes 16777232 | tf_op jit(solution)/shard_map/all_gather | solution.py:81
  944.3 14.5 copy_bitcast_fusion.2
  958.8 6.4 gather_fusion.3
  965.2 1.7 fusion.28
  966.9 11.3 broadcast.314
  978.2 2.6 broadcast.315
  980.7 20.4 %while.91 = (s32[]{:T(128)}, f32[32,2048,128]{2,0,1:T(8,128)}, f32[32,256,128]{2,0,1:T(8,128)}, s32[]{:T(128)}, s32[64]{0:T(128)S(1)}, /*index=5*/s32[]{:T(128)}...) while((s32[]{:T(128)}, f32[32,2048,128]{2,0,1:T(8,128)}, ...), condition=%wide.region_18.21_spmd.clone, body=%wide.region_15.20_spmd.clone.sunk | while | flops 1049155 | bytes 10487937 | solution.py:69
  981.4 2.7 broadcast_multiply_fusion.9
  984.1 9.0 scatter_fusion.2
  993.1 8.0 scatter_fusion.3
  1001.1 4.4 copy_bitcast_fusion.4
  1005.6 22.6 %copy_bitcast_fusion = f32[32,262144]{1,0:T(8,128)} fusion(f32[32,2048,128]{2,0,1:T(8,128)} %get-tuple-element.613), kind=kLoop, calls=%fused_computation.68 | loop fusion | bytes 67108864 | tf_op jit(solution)/shard_map/reshape | solution.py:86
  1028.2 30.0 %reduce-scatter.11.cloned.1.call-done = f32[32,16384]{1,0:T(8,128)} async-done(((f32[32,32768]{1,0:T(8,128)}), f32[32,16384]{1,0:T(8,128)}) %reduce-scatter.11.cloned.1.call-update) | async-done | bytes 2097168 | tf_op jit(solution)/shard_map/reduce_scatter | solution.py:88
  1058.2 336.9 %reduce-scatter.9.cloned.1.call-done = f32[32,16384]{1,0:T(8,128)} async-done(((f32[32,262144]{1,0:T(8,128)}), f32[32,16384]{1,0:T(8,128)}) %reduce-scatter.9.cloned.1.call-update) | async-done | bytes 2097168 | tf_op jit(solution)/shard_map/reduce_scatter | solution.py:85
  1395.2 2.4 add.221
  1397.6 1.3 copy-done.1
  1398.9 1.8 fusion.53
  1400.7 39.0 %psum.15 = f32[32,32]{1,0:T(8,128)S(1)} all-reduce(f32[32,32]{1,0:T(8,128)S(1)} %fusion.53), channel_id=1, replica_groups=mesh['row'=2,'col'=16] {'row','col'}, use_global_device_ids=true, to_apply=%region_21.24 | all-reduce | flops 1024 | bytes 8192 | tf_op jit(solution)/shard_map/psum | solution.py:95
  1439.8 53.9 %while.94 = (s32[]{:T(128)}, f32[32,32]{1,0:T(8,128)S(1)}, f32[32,32]{0,1:T(8,128)S(1)}, s32[]{:T(128)}, s32[]{:T(128)}) while((s32[]{:T(128)}, f32[32,32]{1,0:T(8,128)S(1)}, f32[32,32]{0,1:T(8,128)S(1)}, s32[]{:T(128)}, s32[]{:T(128)}) %tuple.201), condition=%wide.region_25.28_spmd.clone.clone, body=%wide.region_22.27_spmd.clone.clone.sunk | while | flops 2401 | bytes 8913 | solution.py:26
  1493.7 44.3 %while.95 = (s32[]{:T(128)}, f32[32,32]{1,0:T(8,128)S(1)}, f32[32,32]{1,0:T(8,128)S(1)}, s32[]{:T(128)}, s32[]{:T(128)}) while((s32[]{:T(128)}, f32[32,32]{1,0:T(8,128)S(1)}, f32[32,32]{1,0:T(8,128)S(1)}, s32[]{:T(128)}, s32[]{:T(128)}) %tuple.204), condition=%wide.region_29.32_spmd.clone.clone, body=%wide.region_26.31_spmd.clone.clone.sunk | while | flops 2305 | bytes 6221 | solution.py:43
  1538.1 4.8 fusion.54
  (669 shorter events, 151.3 us)
Async XLA Ops:
  6.5 44.4 %copy-start = (bf16[64,128,128]{2,1,0:T(8,128)(2,1)S(1)}, bf16[64,128,128]{2,1,0:T(8,128)(2,1)}, u32[]{:S(2)}) copy-start(bf16[64,128,128]{2,1,0:T(8,128)(2,1)} %param.21) | copy-start | bytes 6291460
  6.5 4.3 copy-start.3
  6.5 4.4 copy-start.4
  6.5 38.8 %all-gather.5.cloned.1.call-start = ((), (), s32[]{:S(2)}) async-start(), calls=%async_computation.4 | async-start | bytes 3145728 | tf_op jit(solution)/shard_map/all_gather | solution.py:80
  9.4 165.1 %all-gather.7.cloned.1.call-start = ((), (), s32[]{:S(2)}) async-start(), calls=%async_computation.5 | async-start | bytes 17825792 | tf_op jit(solution)/shard_map/all_gather | solution.py:81
  10.2 278.3 %reduce-scatter.7.cloned.1.call-start = ((), (), s32[]{:S(2)}) async-start(), calls=%async_computation.7 | async-start | bytes 6291456 | tf_op jit(solution)/shard_map/reduce_scatter | solution.py:88
  235.8 390.0 %reduce-scatter.5.cloned.1.call-start = ((), (), s32[]{:S(2)}) async-start(), calls=%async_computation.6 | async-start | bytes 35651584 | tf_op jit(solution)/shard_map/reduce_scatter | solution.py:85
  258.4 556.7 %all-gather.9.cloned.1.call-start = ((), (), s32[]{:S(2)}) async-start(), calls=%async_computation.8 | async-start | bytes 3145728 | tf_op jit(solution)/shard_map/all_gather | solution.py:80
  628.2 1.3 copy-start.2
  782.0 162.3 %all-gather.11.cloned.1.call-start = ((), (), s32[]{:S(2)}) async-start(), calls=%async_computation.9 | async-start | bytes 17825792 | tf_op jit(solution)/shard_map/all_gather | solution.py:81
  782.6 275.6 %reduce-scatter.11.cloned.1.call-start = ((), (), s32[]{:S(2)}) async-start(), calls=%async_computation.11 | async-start | bytes 6291456 | tf_op jit(solution)/shard_map/reduce_scatter | solution.py:88
  1005.6 389.6 %reduce-scatter.9.cloned.1.call-start = ((), (), s32[]{:S(2)}) async-start(), calls=%async_computation.10 | async-start | bytes 35651584 | tf_op jit(solution)/shard_map/reduce_scatter | solution.py:85
  1397.6 1.4 copy-start.1
Sparse Core Ops, SparseCore 0:
  9.5 35.8 all-gather.4
  47.6 126.9 all-gather.6
  235.9 52.4 reduce-scatter.6
  293.1 332.6 reduce-scatter.4
  782.1 32.8 all-gather.8
  817.4 126.9 all-gather.10
  1005.7 52.4 reduce-scatter.10
  1062.5 332.6 reduce-scatter.8
where the time goes:
time: 1550 us
  waiting for transfers between devices  1050 us (68%)
  other arithmetic  189 us (12%)
  local copies, waits for them, and re-layouts  153 us (10%)
  blocking collectives  78.1 us (5%)
  loops' own time  48.3 us (3%)
  matrix products  20.5 us (1%)
    reduce_scatter x2, waiting for transfers between devices, per_device(): lax.psum_scatter(row_sums.reshape(vector_count, -1), 'col', scatter_dimen...  674 us
    all_gather x2, waiting for transfers between devices, per_device(): row_panel = lax.all_gather(rounded, 'col', axis=1, tiled=True)  243 us
    psum x2, blocking collectives, per_device(): gram_matrix = lax.psum(local_gram, ('row', 'col')) / N  78.1 us
    all_gather x2, waiting for transfers between devices, per_device(): col_panel = lax.all_gather(rounded, 'row', axis=1, tiled=True)  66.7 us
    reduce_scatter x2, waiting for transfers between devices, per_device(): lax.psum_scatter(col_sums.reshape(vector_count, -1), 'row', scatter_dimen...  60 us
    another operation x2, loops' own time, cholesky_lower(): lax.fori_loop(0, matrix_order, column_step, jnp.zeros_like(gram_matrix))  46.9 us
    reshape x2, local copies, waits for them, and re-layouts, per_device(): row_sums.reshape(vector_count, -1)  45.2 us
    reduce_sum x64, other arithmetic, column_step(): pivot_value = jnp.sqrt(jnp.sum(jnp.where(on_diagonal, residue, 0.0)))  42.8 us
  transfers between devices with their start and end apart: 8, of which 8 were waited for; matrix products, arithmetic and copies ran while one was open for 4% of the time, Pallas kernels for 0%

commit v1 on v0

--- a/solution.py
+++ b/solution.py
@@ -6,6 +6,12 @@
 
 N = 524288
 ITERS = 2
+
+
+def gather_and_add(x, name):
+    parts = lax.all_gather(x, name, axis=0, tiled=False)
+    total = parts.sum(axis=0)
+    return total
 
 
 def cholesky_lower(gram_matrix):
@@ -92,7 +98,7 @@
         local_gram = jnp.dot(
             product, product.T, precision=lax.Precision.HIGHEST, preferred_element_type=jnp.float32
         )
-        gram_matrix = lax.psum(local_gram, ("row", "col")) / N
+        gram_matrix = gather_and_add(local_gram, ("row", "col")) / N
         inverse = lower_inverse(cholesky_lower(gram_matrix))
         vectors = jnp.dot(
             inverse, product, precision=lax.Precision.HIGHEST, preferred_element_type=jnp.float32

time: 1550 us -> 1550 us (level)
    all_gather x0 -> x2, blocking collectives: none -> 82 us  [gather_and_add(): parts = lax.all_gather(x, name, axis=0, tiled=False)]
    psum x2 -> x0, blocking collectives: 78.1 us -> none  [per_device(): gram_matrix = lax.psum(local_gram, ('row', 'col')) / N]
where the time goes in v1:
time: 1550 us
  waiting for transfers between devices  1040 us (67%)
  other arithmetic  190 us (12%)
  local copies, waits for them, and re-layouts  153 us (10%)
  blocking collectives  82 us (5%)
  loops' own time  48.3 us (3%)
  matrix products  20.5 us (1%)
    reduce_scatter x2, waiting for transfers between devices, per_device(): lax.psum_scatter(row_sums.reshape(vector_count, -1), 'col', scatter_dimen...  674 us
    all_gather x2, waiting for transfers between devices, per_device(): row_panel = lax.all_gather(rounded, 'col', axis=1, tiled=True)  243 us
    all_gather x2, blocking collectives, gather_and_add(): parts = lax.all_gather(x, name, axis=0, tiled=False)  82 us
    all_gather x2, waiting for transfers between devices, per_device(): col_panel = lax.all_gather(rounded, 'row', axis=1, tiled=True)  63.2 us
    reduce_scatter x2, waiting for transfers between devices, per_device(): lax.psum_scatter(col_sums.reshape(vector_count, -1), 'row', scatter_dimen...  60 us
    another operation x2, loops' own time, cholesky_lower(): lax.fori_loop(0, matrix_order, column_step, jnp.zeros_like(gram_matrix))  46.9 us
    reshape x2, local copies, waits for them, and re-layouts, per_device(): row_sums.reshape(vector_count, -1)  45.2 us
    reduce_sum x64, other arithmetic, column_step(): pivot_value = jnp.sqrt(jnp.sum(jnp.where(on_diagonal, residue, 0.0)))  42.8 us
  transfers between devices with their start and end apart: 8, of which 8 were waited for; matrix products, arithmetic and copies ran while one was open for 4% of the time, Pallas kernels for 0%

profile of v1, /device:TPU:0, one launch (start us, length us, event | category | flops | bytes accessed | tf_op | source)
XLA Modules:
  0.0 1550.3 jit_solution(10772618701418687809)
XLA Ops:
  6.5 2.8 convert_element_type.66
  9.4 0.7 all-gather.9.cloned.1.call-update
  11.0 34.4 %all-gather.7.cloned.1.call-done = bf16[32,32768]{1,0:T(8,128)(2,1)} async-done(((bf16[32,16384]{1,0:T(8,128)(2,1)}), bf16[32,32768]{1,0:T(8,128)(2,1)}) %all-gather.7.cloned.1.call-update) | async-done | bytes 2097168 | tf_op jit(solution)/shard_map/all_gather | solution.py:86
  45.4 3.3 copy_bitcast_fusion.7
  48.6 2.2 gather_fusion
  50.9 2.2 fusion.34
  53.1 121.4 %all-gather.9.cloned.1.call-done = bf16[32,262144]{1,0:T(8,128)(2,1)} async-done(((bf16[32,16384]{1,0:T(8,128)(2,1)}), bf16[32,262144]{1,0:T(8,128)(2,1)}) %all-gather.9.cloned.1.call-update) | async-done | bytes 16777232 | tf_op jit(solution)/shard_map/all_gather | solution.py:87
  174.5 14.5 copy_bitcast_fusion.3
  189.0 6.4 gather_fusion.1
  195.4 1.7 fusion.32
  197.1 11.3 broadcast.314.clone
  208.4 2.6 broadcast.315.clone
  210.9 20.4 %while.90 = (s32[]{:T(128)}, f32[32,2048,128]{2,0,1:T(8,128)}, f32[32,256,128]{2,0,1:T(8,128)}, s32[]{:T(128)}, s32[64]{0:T(128)S(1)}, /*index=5*/s32[]{:T(128)}...) while((s32[]{:T(128)}, f32[32,2048,128]{2,0,1:T(8,128)}, ...), condition=%wide.region_3.6_spmd.clone, body=%wide.region_0.5_spmd.clone.sunk | while | flops 1049155 | bytes 10487937 | solution.py:75
  211.6 2.7 broadcast_multiply_fusion.8
  214.3 9.0 scatter_fusion
  223.3 8.0 scatter_fusion.1
  231.3 4.4 copy_bitcast_fusion.5
  235.8 22.6 %copy_bitcast_fusion.1 = f32[32,262144]{1,0:T(8,128)} fusion(f32[32,2048,128]{2,0,1:T(8,128)} %get-tuple-element.609), kind=kLoop, calls=%fused_computation.69 | loop fusion | bytes 67108864 | tf_op jit(solution)/shard_map/reshape | solution.py:92
  258.5 30.0 %reduce-scatter.7.cloned.1.call-done = f32[32,16384]{1,0:T(8,128)} async-done(((f32[32,32768]{1,0:T(8,128)}), f32[32,16384]{1,0:T(8,128)}) %reduce-scatter.7.cloned.1.call-update) | async-done | bytes 2097168 | tf_op jit(solution)/shard_map/reduce_scatter | solution.py:94
  288.4 337.4 %reduce-scatter.5.cloned.1.call-done = f32[32,16384]{1,0:T(8,128)} async-done(((f32[32,262144]{1,0:T(8,128)}), f32[32,16384]{1,0:T(8,128)}) %reduce-scatter.5.cloned.1.call-update) | async-done | bytes 2097168 | tf_op jit(solution)/shard_map/reduce_scatter | solution.py:91
  625.8 2.4 add.216
  628.2 1.3 copy-done.2
  629.5 1.8 fusion.52
  631.3 41.0 %all-gather = f32[1024,32]{1,0:T(8,128)S(1)} all-gather(f32[32,32]{1,0:T(8,128)S(1)} %fusion.52), channel_id=2, replica_groups=mesh['row'=2,'col'=16] {'row','col'}, dimensions={0}, use_global_device_ids=true | all-gather | bytes 135168 | tf_op jit(solution)/shard_map/all_gather | solution.py:12
  672.5 58.1 %while.92 = (s32[]{:T(128)}, f32[32,32]{1,0:T(8,128)S(1)}, f32[32,32]{0,1:T(8,128)S(1)}, s32[]{:T(128)}, s32[]{:T(128)}) while((s32[]{:T(128)}, f32[32,32]{1,0:T(8,128)S(1)}, f32[32,32]{0,1:T(8,128)S(1)}, s32[]{:T(128)}, s32[]{:T(128)}) %tuple.192), condition=%wide.region_10.13_spmd.clone.clone, body=%wide.region_7.12_spmd.clone.clone.sunk | while | flops 2401 | bytes 8913 | solution.py:32
  672.6 0.7 fusion.88
  674.3 0.7 fusion.88
  676.2 0.7 fusion.88
  678.0 0.7 fusion.88
  679.8 0.7 fusion.88
  681.6 0.7 fusion.88
  683.4 0.7 fusion.88
  694.4 0.7 fusion.88
  699.8 0.7 fusion.88
  705.3 0.7 fusion.88
  710.7 0.7 fusion.88
  728.9 0.7 fusion.88
  730.6 49.0 %while.93 = (s32[]{:T(128)}, f32[32,32]{1,0:T(8,128)S(1)}, f32[32,32]{1,0:T(8,128)S(1)}, s32[]{:T(128)}, s32[]{:T(128)}) while((s32[]{:T(128)}, f32[32,32]{1,0:T(8,128)S(1)}, f32[32,32]{1,0:T(8,128)S(1)}, s32[]{:T(128)}, s32[]{:T(128)}) %tuple.195), condition=%wide.region_14.17_spmd.clone.clone, body=%wide.region_11.16_spmd.clone.clone.sunk | while | flops 2305 | bytes 6221 | solution.py:49
  779.6 4.4 convolution_convert_fusion
  784.8 28.8 %all-gather.11.cloned.1.call-done = bf16[32,32768]{1,0:T(8,128)(2,1)} async-done(((bf16[32,16384]{1,0:T(8,128)(2,1)}), bf16[32,32768]{1,0:T(8,128)(2,1)}) %all-gather.11.cloned.1.call-update) | async-done | bytes 2097168 | tf_op jit(solution)/shard_map/all_gather | solution.py:86
  813.7 3.3 copy_bitcast_fusion.6
  816.9 2.2 gather_fusion.2
  819.2 2.2 fusion.30
  821.4 121.5 %all-gather.13.cloned.1.call-done = bf16[32,262144]{1,0:T(8,128)(2,1)} async-done(((bf16[32,16384]{1,0:T(8,128)(2,1)}), bf16[32,262144]{1,0:T(8,128)(2,1)}) %all-gather.13.cloned.1.call-update) | async-done | bytes 16777232 | tf_op jit(solution)/shard_map/all_gather | solution.py:87
  942.9 14.5 copy_bitcast_fusion.2
  957.4 6.4 gather_fusion.3
  963.8 1.7 fusion.28
  965.5 11.3 broadcast.314
  976.8 2.6 broadcast.315
  979.3 20.4 %while.91 = (s32[]{:T(128)}, f32[32,2048,128]{2,0,1:T(8,128)}, f32[32,256,128]{2,0,1:T(8,128)}, s32[]{:T(128)}, s32[64]{0:T(128)S(1)}, /*index=5*/s32[]{:T(128)}...) while((s32[]{:T(128)}, f32[32,2048,128]{2,0,1:T(8,128)}, ...), condition=%wide.region_18.21_spmd.clone, body=%wide.region_15.20_spmd.clone.sunk | while | flops 1049155 | bytes 10487937 | solution.py:75
  980.0 2.7 broadcast_multiply_fusion.9
  982.7 9.0 scatter_fusion.2
  991.7 8.0 scatter_fusion.3
  999.7 4.4 copy_bitcast_fusion.4
  1004.2 22.6 %copy_bitcast_fusion = f32[32,262144]{1,0:T(8,128)} fusion(f32[32,2048,128]{2,0,1:T(8,128)} %get-tuple-element.613), kind=kLoop, calls=%fused_computation.68 | loop fusion | bytes 67108864 | tf_op jit(solution)/shard_map/reshape | solution.py:92
  1026.8 30.0 %reduce-scatter.11.cloned.1.call-done = f32[32,16384]{1,0:T(8,128)} async-done(((f32[32,32768]{1,0:T(8,128)}), f32[32,16384]{1,0:T(8,128)}) %reduce-scatter.11.cloned.1.call-update) | async-done | bytes 2097168 | tf_op jit(solution)/shard_map/reduce_scatter | solution.py:94
  1056.8 336.9 %reduce-scatter.9.cloned.1.call-done = f32[32,16384]{1,0:T(8,128)} async-done(((f32[32,262144]{1,0:T(8,128)}), f32[32,16384]{1,0:T(8,128)}) %reduce-scatter.9.cloned.1.call-update) | async-done | bytes 2097168 | tf_op jit(solution)/shard_map/reduce_scatter | solution.py:91
  1393.7 2.4 add.217
  1396.2 1.3 copy-done.1
  1397.5 1.8 fusion.53
  1399.3 41.0 %all-gather.1 = f32[1024,32]{1,0:T(8,128)S(1)} all-gather(f32[32,32]{1,0:T(8,128)S(1)} %fusion.53), channel_id=3, replica_groups=mesh['row'=2,'col'=16] {'row','col'}, dimensions={0}, use_global_device_ids=true | all-gather | bytes 135168 | tf_op jit(solution)/shard_map/all_gather | solution.py:12
  1440.4 53.9 %while.94 = (s32[]{:T(128)}, f32[32,32]{1,0:T(8,128)S(1)}, f32[32,32]{0,1:T(8,128)S(1)}, s32[]{:T(128)}, s32[]{:T(128)}) while((s32[]{:T(128)}, f32[32,32]{1,0:T(8,128)S(1)}, f32[32,32]{0,1:T(8,128)S(1)}, s32[]{:T(128)}, s32[]{:T(128)}) %tuple.201), condition=%wide.region_25.28_spmd.clone.clone, body=%wide.region_22.27_spmd.clone.clone.sunk | while | flops 2401 | bytes 8913 | solution.py:32
  1494.4 44.3 %while.95 = (s32[]{:T(128)}, f32[32,32]{1,0:T(8,128)S(1)}, f32[32,32]{1,0:T(8,128)S(1)}, s32[]{:T(128)}, s32[]{:T(128)}) while((s32[]{:T(128)}, f32[32,32]{1,0:T(8,128)S(1)}, f32[32,32]{1,0:T(8,128)S(1)}, s32[]{:T(128)}, s32[]{:T(128)}) %tuple.204), condition=%wide.region_29.32_spmd.clone.clone, body=%wide.region_26.31_spmd.clone.clone.sunk | while | flops 2305 | bytes 6221 | solution.py:49
  1538.7 4.8 fusion.54
  (671 shorter events, 151.4 us)
Async XLA Ops:
  6.5 44.4 %copy-start = (bf16[64,128,128]{2,1,0:T(8,128)(2,1)S(1)}, bf16[64,128,128]{2,1,0:T(8,128)(2,1)}, u32[]{:S(2)}) copy-start(bf16[64,128,128]{2,1,0:T(8,128)(2,1)} %param.21) | copy-start | bytes 6291460
  6.5 4.3 copy-start.3
  6.5 4.4 copy-start.4
  6.5 38.8 %all-gather.7.cloned.1.call-start = ((), (), s32[]{:S(2)}) async-start(), calls=%async_computation.4 | async-start | bytes 3145728 | tf_op jit(solution)/shard_map/all_gather | solution.py:86
  9.4 165.1 %all-gather.9.cloned.1.call-start = ((), (), s32[]{:S(2)}) async-start(), calls=%async_computation.5 | async-start | bytes 17825792 | tf_op jit(solution)/shard_map/all_gather | solution.py:87
  10.2 278.3 %reduce-scatter.7.cloned.1.call-start = ((), (), s32[]{:S(2)}) async-start(), calls=%async_computation.7 | async-start | bytes 6291456 | tf_op jit(solution)/shard_map/reduce_scatter | solution.py:94
  235.8 390.0 %reduce-scatter.5.cloned.1.call-start = ((), (), s32[]{:S(2)}) async-start(), calls=%async_computation.6 | async-start | bytes 35651584 | tf_op jit(solution)/shard_map/reduce_scatter | solution.py:91
  258.4 555.2 %all-gather.11.cloned.1.call-start = ((), (), s32[]{:S(2)}) async-start(), calls=%async_computation.8 | async-start | bytes 3145728 | tf_op jit(solution)/shard_map/all_gather | solution.py:86
  628.2 1.3 copy-start.2
  784.0 158.9 %all-gather.13.cloned.1.call-start = ((), (), s32[]{:S(2)}) async-start(), calls=%async_computation.9 | async-start | bytes 17825792 | tf_op jit(solution)/shard_map/all_gather | solution.py:87
  784.6 272.2 %reduce-scatter.11.cloned.1.call-start = ((), (), s32[]{:S(2)}) async-start(), calls=%async_computation.11 | async-start | bytes 6291456 | tf_op jit(solution)/shard_map/reduce_scatter | solution.py:94
  1004.2 389.6 %reduce-scatter.9.cloned.1.call-start = ((), (), s32[]{:S(2)}) async-start(), calls=%async_computation.10 | async-start | bytes 35651584 | tf_op jit(solution)/shard_map/reduce_scatter | solution.py:91
  1396.2 1.4 copy-start.1
Sparse Core Ops, SparseCore 0:
  9.5 35.8 all-gather.6
  47.6 126.9 all-gather.8
  235.9 52.4 reduce-scatter.6
  293.1 332.6 reduce-scatter.4
  784.2 29.4 all-gather.10
  816.0 126.9 all-gather.12
  1004.3 52.4 reduce-scatter.10
  1061.1 332.6 reduce-scatter.8
